TPU v7x, 1024 devices: a whole 4x4x32 slice. The times are simulated.
1024 devices in a mesh: pb: 128 (over y, z), row: 8 (over x, core).
Axes of the slice: x: 4, y: 4, z: 32, core: 2. Of those that a mesh axis runs over, the one named last changes fastest.
Arguments:
- orbitals: bfloat16 [128, 1280, 128], P('pb', 'row'), may hold values from -4 to 4
- interaction: bfloat16 [2, 128, 1280, 1280], P(None, 'pb', 'row'), may hold values from -0.078125 to 0.078125
- pair_list: int32 [128, 3, 2], P('pb'), may hold values from 0 to 127, as said below
- flag_list: int32 [128, 3], P('pb'), may hold values from 0 to 1
- pair_counts: int32 [128], P('pb'), may hold values from 1 to 3, as said below
Outputs:
- exchange_terms: float32 [128, 3, 1280, 128], P('pb', None, 'row')
Inputs may be any that keep to these rules, and one draw needn't show every extreme that they name: pair_list[q, s, 1] = (pair_list[q, s, 0] - q) mod 128. `pair_counts`: some q has all 3 slots live.
All inputs are finite; a program needn't handle non-finite values.
Results may differ from a plain program's by a relative error of at most 0.0029.
Values may be sent and summed in bfloat16 or wider, within the bound.
A program may use at most 32 MiB of HBM per device.

v0:
```python
import jax
import jax.numpy as jnp
from jax import lax
from jax.sharding import PartitionSpec as P


def rotate_parts(block):
    half_width = block.shape[1] // 2
    return jnp.concatenate([block[:, half_width:], -block[:, :half_width]], axis=1)


def apply_kernel(kern_real, kern_imag, target):
    half_width = target.shape[1] // 2
    prod_real = jnp.dot(kern_real, target, preferred_element_type=jnp.float32)
    prod_imag = jnp.dot(kern_imag, target, preferred_element_type=jnp.float32)
    return jnp.concatenate(
        [
            prod_real[:, :half_width] - prod_imag[:, half_width:],
            prod_real[:, half_width:] + prod_imag[:, :half_width],
        ],
        axis=1,
    )


def density(local_rows, all_rows):
    dens_real = jnp.dot(local_rows, all_rows.T, preferred_element_type=jnp.float32)
    dens_imag = jnp.dot(rotate_parts(local_rows), all_rows.T, preferred_element_type=jnp.float32)
    return (dens_real, dens_imag)


def shards(orbitals, interaction, pair_list, flag_list, pair_counts):
    full_width = orbitals.shape[2]
    half_width = full_width // 2
    slot_total = pair_list.shape[1]
    wanted = jnp.stack([pair_list[0, :, 0], pair_list[0, :, 1]])
    shard_piece = lax.all_gather(orbitals, "pb", axis=0, tiled=True)
    indices = jnp.arange(shard_piece.shape[0], dtype=jnp.int32)
    select = (wanted[:, :, None] == indices[None, None, :]).astype(jnp.bfloat16)
    chosen = jnp.einsum(
        "spi,ird->sprd", select, shard_piece, preferred_element_type=jnp.float32
    ).astype(jnp.bfloat16)
    all_rows = lax.all_gather(chosen, "row", axis=2, tiled=True)
    w_real = interaction[0, 0]
    w_imag = interaction[1, 0]
    active = jnp.arange(slot_total) < pair_counts[0]
    adjoint = flag_list[0] == 1
    forward_parts = []
    real_list = []
    imag_list = []
    for slot_index in range(slot_total):
        dens_real, dens_imag = density(chosen[1, slot_index], all_rows[1, slot_index])
        kern_real = (w_real * dens_real - w_imag * dens_imag).astype(jnp.bfloat16)
        kern_imag = (w_real * dens_imag + w_imag * dens_real).astype(jnp.bfloat16)
        keep_forward = jnp.logical_and(active[slot_index], jnp.logical_not(adjoint[slot_index]))
        keep_adjoint = jnp.logical_and(active[slot_index], adjoint[slot_index]).astype(jnp.bfloat16)
        forward_parts.append(
            apply_kernel(kern_real, kern_imag, all_rows[0, slot_index])
            * keep_forward.astype(jnp.float32)
        )
        real_list.append(kern_real * keep_adjoint)
        imag_list.append(kern_imag * keep_adjoint)
    stack_real = jnp.stack(real_list)
    stack_imag = jnp.stack(imag_list)
    prod_real = jnp.einsum(
        "prc,prd->cpd", stack_real, chosen[0], preferred_element_type=jnp.float32
    )
    prod_imag = jnp.einsum(
        "prc,prd->cpd", stack_imag, chosen[0], preferred_element_type=jnp.float32
    )
    summed = lax.psum_scatter(
        jnp.concatenate(
            [
                prod_real[..., :half_width] + prod_imag[..., half_width:],
                prod_real[..., half_width:] - prod_imag[..., :half_width],
            ],
            axis=2,
        ),
        "row",
        scatter_dimension=0,
        tiled=True,
    )
    output = jnp.stack(forward_parts) + jnp.transpose(summed, (1, 0, 2))
    return output[None]


def solution(mesh):
    return jax.shard_map(
        shards,
        mesh=mesh,
        in_specs=(
            P("pb", "row", None),
            P(None, "pb", "row", None),
            P("pb", None, None),
            P("pb", None),
            P("pb"),
        ),
        out_specs=P("pb", None, "row", None),
        check_vma=False,
    )
```

profile of v0, /device:TPU:1, one launch (start us, length us, event | category | flops | bytes accessed | tf_op | source)
XLA Modules:
  0.0 409.8 jit_solution(4205559119546115511)
XLA Ops:
  6.5 0.0 all-gather.3.cloned.1.call-start
  6.5 0.7 all-gather.3.cloned.1.call-update
  7.3 0.0 all-gather.5.cloned.1.call-start
  7.3 0.8 slice_bitcast_fusion.2
  8.1 0.0 copy-start.4
  8.1 269.1 %all-gather.3.cloned.1.call-done = bf16[128,160,128]{2,1,0:T(8,128)(2,1)} async-done(((bf16[1,160,128]{2,1,0:T(8,128)(2,1)}), bf16[128,160,128]{2,1,0:T(8,128)(2,1)}) %all-gather.3.cloned.1.call-update) | async-done | bytes 5242896 | tf_op jit(solution)/shard_map/all_gather | solution.py:36
  277.1 4.8 %fusion.13 = bf16[2,3,160,128]{3,1,2,0:T(4,128)(2,1)} fusion(bf16[128,160,128]{2,1,0:T(8,128)(2,1)} %all-gather.3.cloned.1.call-done, s32[2,3]{1,0:T(2,128)S(1)} %pad_add_fusion), kind=kOutput, calls=%fused_computation.30 | convolution fusion | flops 31580928 | bytes 5488664 | tf_op jit(solution)/shard_map/spi,ird->sprd/dot_general | solution.py:39
  282.0 0.0 all-gather.5.cloned.1.call-update
  282.0 0.0 reduce-scatter.2.cloned.1.call-start
  282.7 0.0 copy-done.4
  282.7 0.6 fusion.101
  283.3 0.6 fusion.102
  287.7 1.3 fusion.97
  289.1 0.1 fusion.98
  289.2 0.1 fusion.100
  289.2 0.1 fusion.99
  289.3 1.0 slice_bitcast_fusion
  290.3 44.0 %all-gather.5.cloned.1.call-done = bf16[2,3,1280,128]{3,1,2,0:T(4,128)(2,1)} async-done(((bf16[2,3,160,128]{3,1,2,0:T(4,128)(2,1)}), bf16[2,3,1280,128]{3,1,2,0:T(4,128)(2,1)}) %all-gather.5.cloned.1.call-update) | async-done | bytes 1966096 | tf_op jit(solution)/shard_map/all_gather | solution.py:42
  334.3 7.1 %fusion.96 = (bf16[1,1,1280,128]{3,1,2,0:T(2,128)(2,1)S(1)}, bf16[1,1,1280,128]{3,1,2,0:T(2,128)(2,1)S(1)}, bf16[1,1,1280,128]{3,1,2,0:T(2,128)(2,1)S(1)}, bf16[...) fusion(bf16[2,3,1280,128]{3,1,2,0:T(4,128)(2,1)} %all-gather.5.clo, ...), kind=kLoop, calls=%fused_computation.133 | loop fusion | bytes 3932160 | tf_op jit(solution)/shard_map/slice | solution.py:57
  341.5 0.0 copy-start.3
  341.5 0.3 fusion.42
  341.8 0.3 fusion.40
  342.1 0.3 fusion.32
  342.4 0.2 copy-done.3
  342.6 0.5 multiply_bitcast_fusion.3
  343.1 0.3 fusion.48
  343.4 1.7 multiply_bitcast_fusion.5
  345.2 0.8 convolution_bitcast_fusion.1
  346.0 0.8 convolution_bitcast_fusion
  346.8 1.1 slice_add_fusion
  347.9 1.9 pad_maximum_fusion
  349.8 0.0 reduce-scatter.2.cloned.1.call-update
  353.5 0.0 copy-start.2
  353.6 0.0 copy-start.1
  353.6 0.3 fusion.30
  353.8 0.0 copy-start
  353.8 0.3 fusion.28
  354.1 0.1 fusion.68
  354.2 0.1 maximum_multiply_fusion.2
  354.3 0.2 copy-done.2
  354.5 0.3 fusion.46
  354.8 0.0 copy-done.1
  354.8 0.3 fusion.44
  355.1 0.1 fusion.72
  355.2 0.1 maximum_multiply_fusion
  355.3 0.0 copy-done
  355.3 0.3 fusion.36
  355.6 0.3 fusion.38
  355.8 0.1 fusion.70
  356.0 0.1 maximum_multiply_fusion.1
  356.1 45.6 %reduce-scatter.2.cloned.1.call-done = f32[160,3,128]{2,0,1:T(8,128)} async-done(((f32[1280,3,128]{2,0,1:T(8,128)}), f32[160,3,128]{2,0,1:T(8,128)}) %reduce-scatter.2.cloned.1.call-update) | async-done | bytes 245776 | tf_op jit(solution)/shard_map/reduce_scatter | solution.py:70
  401.6 1.7 fusion.52
  (5 shorter events, 0.0 us)
Async XLA Ops:
  6.5 270.6 %all-gather.3.cloned.1.call-start = ((), (), s32[]{:S(2)}) async-start(), calls=%async_computation.1 | async-start | bytes 5283840 | tf_op jit(solution)/shard_map/all_gather | solution.py:36
  7.3 327.1 %all-gather.5.cloned.1.call-start = ((), (), s32[]{:S(2)}) async-start(), calls=%async_computation.2 | async-start | bytes 2949120 | tf_op jit(solution)/shard_map/all_gather | solution.py:42
  8.1 274.6 %copy-start.4 = (s32[1,3]{1,0:T(1,128)S(1)}, s32[1,3]{1,0:T(1,128)}, u32[]{:S(2)}) copy-start(s32[1,3]{1,0:T(1,128)} %param.8) | copy-start | bytes 40
  282.0 119.7 %reduce-scatter.2.cloned.1.call-start = ((), (), s32[]{:S(2)}) async-start(), calls=%async_computation.3 | async-start | bytes 2211840 | tf_op jit(solution)/shard_map/reduce_scatter | solution.py:70
  341.5 1.1 copy-start.3
  353.5 1.0 copy-start.2
  353.6 1.3 copy-start.1
  353.8 1.5 copy-start
Sparse Core Ops, SparseCore 0:
  11.4 265.6 all-gather.2
  282.1 52.1 all-gather.4
  349.9 51.6 reduce-scatter.1
where the time goes:
time: 410 us
  waiting for transfers between devices  359 us (88%)
  between operations  21.5 us (5%)
  local copies, waits for them, and re-layouts  12 us (3%)
  matrix products  11.4 us (3%)
  other arithmetic  5.49 us (1%)
    all_gather x1, waiting for transfers between devices, shards(): shard_piece = lax.all_gather(orbitals, 'pb', axis=0, tiled=True)  269 us
    reduce_scatter x1, waiting for transfers between devices, shards(): lax.psum_scatter(jnp.concatenate([prod_real[..., :half_width] + prod_imag...  45.6 us
    all_gather x1, waiting for transfers between devices, shards(): all_rows = lax.all_gather(chosen, 'row', axis=2, tiled=True)  44 us
  transfers between devices with their start and end apart: 3, of which 3 were waited for; matrix products, arithmetic and copies ran while one was open for 2% of the time, Pallas kernels for 0%

commit v1 on v0

v1 whole, which is shorter than its diff:
```python
import functools

import jax
import jax.numpy as jnp
from jax import lax
from jax.experimental import pallas as pl
from jax.experimental.pallas import tpu as pltpu
from jax.sharding import PartitionSpec as P

MESH = pl.DeviceIdType.MESH
NY = 4
CORES = 2
CHUNKS = 2


def gather_kernel(
    ny, nz, nx,
    pair_ref, orb_ref, w_ref,
    full_ref, wcol_ref,
    ring, chosen, wsend, idx_send, idx_all, idx_smem,
    idx_ss, idx_rs, piece_ss, piece_rs, z_ss, z_rs, y_ss, y_rs,
    x_ss, x_rs, hop_ss, hop_rs, core_ss, core_rs, w_ss, w_rs, local_sem,
):
    slots = pair_ref.shape[1]
    wanted = 2 * slots
    pb = lax.axis_index("pb")
    row = lax.axis_index("row")
    y, z = lax.div(pb, nz), lax.rem(pb, nz)
    x, core = lax.div(row, CORES), lax.rem(row, CORES)
    rows = nx * CORES

    def y_peer(d):
        return lax.rem(y + d, ny)

    def z_peer(d):
        return lax.rem(z + d + nz, nz)

    def row_peer(d):
        return lax.rem(row + d, rows)

    def remote(src, dst, ss, rs, to_pb, to_row):
        return pltpu.make_async_remote_copy(
            src_ref=src, dst_ref=dst, send_sem=ss, recv_sem=rs,
            device_id=(to_pb, to_row), device_id_type=MESH,
        )

    barrier = pltpu.get_barrier_semaphore()
    partners = [(y_peer(d) * nz + z, row) for d in range(1, ny)]
    z_steps = (1, -1) if nz > 2 else (1,)
    partners += [(y * nz + z_peer(d), row) for d in z_steps]
    partners += [(pb, row_peer(d)) for d in range(1, rows)]
    for partner in partners:
        pl.semaphore_signal(barrier, inc=1, device_id=partner, device_id_type=MESH)
    pl.semaphore_wait(barrier, len(partners))

    def piece_copy(d):
        to = y_peer(d)
        return remote(
            orb_ref.at[to], ring.at[z, y], piece_ss.at[d - 1], piece_rs.at[d - 1], to * nz + z, row
        )

    for d in range(1, ny):
        piece_copy(d).start()

    lane = lax.broadcasted_iota(jnp.int32, idx_send.shape, 1)
    table = jnp.zeros(idx_send.shape, jnp.int32)
    for j in range(wanted):
        table = jnp.where(lane == j, pair_ref[0, j % slots, j // slots], table)
    idx_send[...] = table
    idx_all[y] = table
    ring[z, y] = orb_ref[y]

    def idx_copy(d):
        to = y_peer(d)
        return remote(
            idx_send, idx_all.at[y], idx_ss.at[d - 1], idx_rs.at[d - 1], to * nz + z, row
        )

    for d in range(1, ny):
        idx_copy(d).start()

    for d in range(1, ny):
        piece_copy(d).wait_recv()

    half = nz // 2
    width = ny // CHUNKS

    def z_copy(way, step, part):
        block = lax.rem(z - step + nz, nz) if way == 0 else lax.rem(z + step, nz)
        view = ring.at[block, pl.ds(part * width, width)]
        return remote(
            view, view, z_ss.at[way, step, part], z_rs.at[way, step, part],
            y * nz + z_peer(1 if way == 0 else -1), row,
        )

    def last(way, part):
        return (part < CHUNKS // 2) == (way == 0)

    pairs = [(way, part) for part in range(CHUNKS) for way in range(2)]
    for way, part in pairs:
        if half > 1 or last(way, part):
            z_copy(way, 0, part).start()

    span = wsend.shape[-1]
    for p in range(rows):
        wsend[p] = w_ref[:, :, p * span : (p + 1) * span]

    def w_copy(d):
        to = row_peer(d)
        return remote(wsend.at[to], wcol_ref.at[row], w_ss.at[d - 1], w_rs.at[d - 1], pb, to)

    for d in range(1, rows):
        w_copy(d).start()
    own_columns = pltpu.make_async_copy(wsend.at[row], wcol_ref.at[row], local_sem.at[0])
    own_columns.start()

    def z_step(step, carry):
        for way, part in pairs:
            z_copy(way, step - 1, part).wait_recv()
            z_copy(way, step, part).start()
        return carry

    if half > 1:
        lax.fori_loop(1, half - 1, z_step, 0)
        for way, part in pairs:
            z_copy(way, half - 2, part).wait_recv()
            if last(way, part):
                z_copy(way, half - 1, part).start()

    for d in range(1, ny):
        idx_copy(d).wait_recv()
    to_smem = pltpu.make_async_copy(idx_all, idx_smem, local_sem.at[1])
    to_smem.start()
    to_smem.wait()

    for way, part in pairs:
        if last(way, part):
            z_copy(way, half - 1, part).wait_recv()

    def y_copy(d):
        to = y_peer(d)
        return remote(
            chosen.at[d - 1], full_ref.at[:, row, y], y_ss.at[d - 1], y_rs.at[d - 1], to * nz + z, row
        )

    for d in range(1, ny):
        to = y_peer(d)
        for j in range(wanted):
            k = idx_smem[to, 0, j]
            chosen[d - 1, j] = ring[lax.rem(k, nz), lax.div(k, nz)]
        y_copy(d).start()
    for j in range(wanted):
        k = idx_smem[y, 0, j]
        full_ref[j, row, y] = ring[lax.rem(k, nz), lax.div(k, nz)]
    for d in range(1, ny):
        y_copy(d).wait_recv()

    other = 1 - core

    def part_of(part, at):
        return full_ref.at[pl.ds(part * slots, slots), at]

    def at_x(d):
        return lax.rem(x + d + nx, nx) * CORES + core

    def x_copy(way, part):
        view = part_of(part, row)
        return remote(
            view, view, x_ss.at[way, part], x_rs.at[way, part], pb, at_x(1 if way == 0 else -1)
        )

    def hop_copy(way):
        view = part_of(1 - way, at_x(-1 if way == 0 else 1))
        return remote(
            view, view, hop_ss.at[way], hop_rs.at[way], pb, at_x(1 if way == 0 else -1)
        )

    def core_copy(d, part):
        view = part_of(part, at_x(d))
        return remote(
            view, view, core_ss.at[d, part], core_rs.at[d, part], pb, x * CORES + other
        )

    if nx == 4:
        for part in (1, 0):
            for way in range(2):
                x_copy(way, part).start()
        for part in (1, 0):
            core_copy(0, part).start()
        for part in (1, 0):
            for way in range(2):
                x_copy(way, part).wait_recv()
                if part == 1 - way:
                    hop_copy(way).start()
                core_copy(3 if way == 0 else 1, part).start()
        for way in range(2):
            hop_copy(way).wait_recv()
            core_copy(2, 1 - way).start()
    else:
        for part in (1, 0):
            core_copy(0, part).start()
    for d in range(nx):
        for part in (1, 0):
            core_copy(d, part).wait_recv()

    own_columns.wait()
    for d in range(1, rows):
        w_copy(d).wait()
    for d in range(1, ny):
        piece_copy(d).wait_send()
        idx_copy(d).wait_send()
        y_copy(d).wait_send()

    def z_drain(step, carry):
        for way, part in pairs:
            z_copy(way, step, part).wait_send()
        return carry

    lax.fori_loop(0, half - 1, z_drain, 0)
    for way, part in pairs:
        if last(way, part):
            z_copy(way, half - 1, part).wait_send()
    if nx == 4:
        for part in (1, 0):
            for way in range(2):
                x_copy(way, part).wait_send()
        for way in range(2):
            hop_copy(way).wait_send()
    for d in range(nx):
        for part in (1, 0):
            core_copy(d, part).wait_send()


def gather(ny, pb_total, rows, pair_list, orbitals, w):
    nz, nx = pb_total // ny, rows // CORES
    slots = pair_list.shape[1]
    piece, width = orbitals.shape[1:]
    span = w.shape[2] // rows
    dma = pltpu.SemaphoreType.DMA
    half = nz // 2
    vmem = pl.BlockSpec(memory_space=pltpu.VMEM)
    sent = 12 * orbitals.size * 2
    return pl.pallas_call(
        functools.partial(gather_kernel, ny, nz, nx),
        out_shape=(
            jax.ShapeDtypeStruct((2 * slots, rows, ny, piece, width), jnp.bfloat16),
            jax.ShapeDtypeStruct((rows, 2, w.shape[1], span), jnp.bfloat16),
        ),
        in_specs=[pl.BlockSpec(memory_space=pltpu.SMEM), vmem, vmem],
        out_specs=(vmem, vmem),
        scratch_shapes=[
            pltpu.VMEM((nz, ny, piece, width), jnp.bfloat16),
            pltpu.VMEM((ny - 1, 2 * slots, piece, width), jnp.bfloat16),
            pltpu.VMEM((rows, 2, w.shape[1], span), jnp.bfloat16),
            pltpu.VMEM((8, 128), jnp.int32),
            pltpu.VMEM((ny, 8, 128), jnp.int32),
            pltpu.SMEM((ny, 8, 128), jnp.int32),
            dma((ny - 1,)), dma((ny - 1,)),
            dma((ny - 1,)), dma((ny - 1,)),
            dma((2, half, CHUNKS)), dma((2, half, CHUNKS)),
            dma((ny - 1,)), dma((ny - 1,)),
            dma((2, 2)), dma((2, 2)),
            dma((2,)), dma((2,)),
            dma((nx, 2)), dma((nx, 2)),
            dma((rows - 1,)), dma((rows - 1,)),
            dma((2,)),
        ],
        compiler_params=pltpu.CompilerParams(collective_id=0, has_side_effects=True),
        name="gather_orbitals",
    )(pair_list, orbitals, w)


def dot_t(a, b):
    return lax.dot_general(a, b, (((1,), (1,)), ((), ())), preferred_element_type=jnp.float32)


def rotate(block):
    half = block.shape[1] // 2
    return jnp.concatenate([block[:, half:], -block[:, :half]], axis=1)


def exchange_kernel(flag_ref, count_ref, place_ref, full_ref, w_ref, wcol_ref, out_ref):
    slots, local, width = out_ref.shape
    rows = full_ref.shape[1]
    half = width // 2
    total = w_ref.shape[2]
    tile = 256
    me = place_ref[0]

    for s in range(slots):
        live = s < count_ref[0]
        adjoint = flag_ref[0, s] == 1

        @pl.when(jnp.logical_and(live, jnp.logical_not(adjoint)))
        def _(s=s):
            mine = full_ref[slots + s, pl.ds(pl.multiple_of(me * local, local), local), :]
            turned = rotate(mine)
            prod_re = jnp.zeros((local, width), jnp.float32)
            prod_im = jnp.zeros((local, width), jnp.float32)
            for c in range(total // tile):
                cols = pl.ds(c * tile, tile)
                source = full_ref[slots + s, cols, :]
                target = full_ref[s, cols, :]
                d_re = dot_t(mine, source)
                d_im = dot_t(turned, source)
                w_re = w_ref[0, :, cols].astype(jnp.float32)
                w_im = w_ref[1, :, cols].astype(jnp.float32)
                k_re = (w_re * d_re - w_im * d_im).astype(jnp.bfloat16)
                k_im = (w_re * d_im + w_im * d_re).astype(jnp.bfloat16)
                prod_re += jnp.dot(k_re, target, preferred_element_type=jnp.float32)
                prod_im += jnp.dot(k_im, target, preferred_element_type=jnp.float32)
            out_ref[s, :, :half] = prod_re[:, :half] - prod_im[:, half:]
            out_ref[s, :, half:] = prod_re[:, half:] + prod_im[:, :half]

        @pl.when(jnp.logical_and(live, adjoint))
        def _(s=s):
            mine = full_ref[slots + s, pl.ds(pl.multiple_of(me * local, local), local), :]
            prod_re = jnp.zeros((width, local), jnp.float32)
            prod_im = jnp.zeros((width, local), jnp.float32)
            for p in range(wcol_ref.shape[0]):
                cols = pl.ds(p * local, local)
                source = full_ref[slots + s, cols, :]
                target = full_ref[s, cols, :]
                d_re = dot_t(source, mine)
                d_im = dot_t(rotate(source), mine)
                w_re = wcol_ref[p, 0].astype(jnp.float32)
                w_im = wcol_ref[p, 1].astype(jnp.float32)
                k_re = (w_re * d_re - w_im * d_im).astype(jnp.bfloat16)
                k_im = (w_re * d_im + w_im * d_re).astype(jnp.bfloat16)
                flip = target.T
                prod_re += jnp.dot(flip, k_re, preferred_element_type=jnp.float32)
                prod_im += jnp.dot(flip, k_im, preferred_element_type=jnp.float32)
            top = prod_re[:half] + prod_im[half:]
            bottom = prod_re[half:] - prod_im[:half]
            out_ref[s] = jnp.concatenate([top, bottom], axis=0).T

        @pl.when(jnp.logical_not(live))
        def _(s=s):
            out_ref[s] = jnp.zeros((local, width), jnp.float32)


def exchange(flag_list, pair_counts, place, full, w, wcol):
    slots = full.shape[0] // 2
    local, width = w.shape[1], full.shape[2]
    smem = pl.BlockSpec(memory_space=pltpu.SMEM)
    vmem = pl.BlockSpec(memory_space=pltpu.VMEM)
    return pl.pallas_call(
        exchange_kernel,
        out_shape=jax.ShapeDtypeStruct((slots, local, width), jnp.float32),
        in_specs=[smem, smem, smem, vmem, vmem, vmem],
        out_specs=vmem,
        name="exchange_terms",
    )(flag_list, pair_counts, place, full, w, wcol)


def shards(ny, pb_total, rows, orbitals, interaction, pair_list, flag_list, pair_counts):
    local, width = orbitals.shape[1:]
    w = interaction[:, 0]
    pieces = orbitals.reshape(ny, local // ny, width)
    full, wcol = gather(ny, pb_total, rows, pair_list, pieces, w)
    full = full.reshape(full.shape[0], rows * local, width)
    place = lax.axis_index("row").astype(jnp.int32).reshape(1)
    return exchange(flag_list, pair_counts, place, full, w, wcol)[None]


def solution(mesh, ny=NY):
    return jax.shard_map(
        functools.partial(shards, ny, mesh.shape["pb"], mesh.shape["row"]),
        mesh=mesh,
        in_specs=(
            P("pb", "row", None),
            P(None, "pb", "row", None),
            P("pb", None, None),
            P("pb", None),
            P("pb"),
        ),
        out_specs=P("pb", None, "row", None),
        check_vma=False,
    )
```

time: 410 us -> 103 us (0.25)
  waiting for transfers between devices: 359 us -> 0 us
  Pallas kernels: 0 us -> 101 us
  between operations: 21.5 us -> 0.66 us
  matrix products: 11.4 us -> 0 us
  local copies, waits for them, and re-layouts: 12 us -> 1.34 us
  other arithmetic: 5.49 us -> 0 us
    all_gather x2 -> x0, waiting for transfers between devices: 313 us -> none  [the longest x1 269 us: shards(): shard_piece = lax.all_gather(orbitals, 'pb', axis=0, tiled=True)]
    pallas_call x0 -> x2, Pallas kernels: none -> 101 us  [the longest x1 94.3 us: gather(): pl.pallas_call(functools.partial(gather_kernel, ny, nz, nx), out_shape=(j...]
    reduce_scatter x1 -> x0, waiting for transfers between devices: 45.6 us -> none  [shards(): lax.psum_scatter(jnp.concatenate([prod_real[..., :half_width] + prod_imag...]
    dot_general x15 -> x0, matrix products: 11.4 us -> none  [the longest x1 4.81 us: shards(): jnp.einsum('spi,ird->sprd', select, shard_piece, preferred_element_type=j...]
    slice x4 -> x0, local copies, waits for them, and re-layouts: 9.72 us -> none  [the longest x1 7.15 us: shards(): all_rows[0, slot_index]]
  transfers between devices with their start and end apart: 3 -> 0, of which waited for: 3 -> 0; matrix products, arithmetic and copies ran while one was open for 2% -> 0% of each run, Pallas kernels for 0% -> 0%
where the time goes in v1:
time: 103 us
  Pallas kernels  101 us (98%)
  local copies, waits for them, and re-layouts  1.34 us (1%)
    pallas_call x1, Pallas kernels, gather(): pl.pallas_call(functools.partial(gather_kernel, ny, nz, nx), out_shape=(j...  94.3 us
    pallas_call x1, Pallas kernels, exchange(): pl.pallas_call(exchange_kernel, out_shape=jax.ShapeDtypeStruct((slots, lo...  6.26 us

profile of v1, /device:TPU:1, one launch (start us, length us, event | category | flops | bytes accessed | tf_op | source)
XLA Modules:
  0.0 102.6 jit_solution(14372509571048714547)
XLA Ops:
  0.7 1.3 %copy.6.pair_ref = s32[1,3,2]{2,1,0:T(4,128)} copy(s32[1,3,2]{1,2,0:T(2,128)} %param.7) | data formatting | bytes 48 | tf_op args[2]
  2.0 94.3 %gather_orbitals.1 = (bf16[6,8,4,40,128]{4,3,2,1,0:T(8,128)(2,1)}, bf16[8,2,160,160]{3,2,1,0:T(8,128)(2,1)}) custom-call(s32[1,3,2]{2,1,0:T(4,128)} %copy.6.pair_ref, bf16[4,40,128]{2,1,0:T(8,128)(2,1)} %bitcast.8, bf16[2,160,1280]{2,1,0:T(8,128)(2,1)} %bitcast.5), custom_call_target="tpu_custom_call" | custom-call | tf_op jit(solution)/shard_map/gather_orbitals/pallas_call | solution.py:243
  96.3 6.3 %exchange_terms.1 = f32[3,160,128]{2,1,0:T(8,128)} custom-call(s32[1,3]{1,0:T(1,128)} %flag_ref.1, s32[1]{0:T(128)S(6)} %copy.7.count_ref, s32[1]{0:T(128)} %bitcast.place_ref, bf16[6,1280,128]{2,1,0:T(8,128)(2,1)} %bitcast.7, bf16[2,160,1280]{2,1,0:T(8,128)(2,1)} %bitcast.6, bf16[8,2,160,160]{3,2,1,0:T(8,128)(2,1)} %get-tuple-element.8.wcol_ref), custom_call_target="tpu_custom_call" | custom-call | tf_op jit(solution)/shard_map/exchange_terms/pallas_call | solution.py:347

commit v2 on v1

v2 whole, which is shorter than its diff:
```python
import functools

import jax
import jax.numpy as jnp
from jax import lax
from jax.experimental import pallas as pl
from jax.experimental.pallas import tpu as pltpu
from jax.sharding import PartitionSpec as P

MESH = pl.DeviceIdType.MESH
NY = 4
CORES = 2
LANES = 128
CHUNKS = 2
GROUP = 2


def gather_kernel(
    ny, nz, nx, group,
    pair_ref, orb_ref, w_ref,
    full_ref, wcol_ref,
    ring, chosen, wsend, idx_send, idx_all, idx_smem,
    idx_ss, idx_rs, piece_ss, piece_rs, z_ss, z_rs, sib_ss, sib_rs, own_ss, own_rs, y_ss, y_rs,
    x_ss, x_rs, hop_ss, hop_rs, core_ss, core_rs, w_ss, w_rs, local_sem,
):
    slots = pair_ref.shape[2]
    wanted = 2 * slots
    pb = lax.axis_index("pb")
    row = lax.axis_index("row")
    y, z = lax.div(pb, nz), lax.rem(pb, nz)
    x, core = lax.div(row, CORES), lax.rem(row, CORES)
    rows = nx * CORES
    stops = nz // group
    stop, seat = lax.div(z, group), lax.rem(z, group)
    kind = lax.rem(row, group)
    base = row - kind
    t_z, t_row = stop * group + kind, base + seat
    same = seat == kind
    moved = jnp.logical_not(same)

    def y_peer(d):
        return lax.rem(y + d, ny)

    def z_peer(d):
        return lax.rem(z + d * group + nz, nz)

    def row_peer(d):
        return lax.rem(row + d, rows)

    def remote(src, dst, ss, rs, to_pb, to_row):
        return pltpu.make_async_remote_copy(
            src_ref=src, dst_ref=dst, send_sem=ss, recv_sem=rs,
            device_id=(to_pb, to_row), device_id_type=MESH,
        )

    barrier = pltpu.get_barrier_semaphore()
    partners = [(y_peer(d) * nz + t_z, t_row) for d in range(1, ny)]
    ways = (1, -1) if stops > 2 else (1,)
    partners += [(y * nz + z_peer(d), row) for d in ways]
    partners += [(pb, row_peer(d)) for d in range(1, rows)]
    for partner in partners:
        pl.semaphore_signal(barrier, inc=1, device_id=partner, device_id_type=MESH)

    @pl.when(moved)
    def _():
        pl.semaphore_signal(
            barrier, inc=1, device_id=(y * nz + t_z, t_row), device_id_type=MESH
        )
        pl.semaphore_wait(barrier, len(partners) + 1)

    @pl.when(same)
    def _():
        pl.semaphore_wait(barrier, len(partners))

    def to_swap(src, dst, ss, rs, d):
        return remote(src, dst, ss.at[d], rs.at[d], y_peer(d) * nz + t_z, t_row)

    def piece_copy(d):
        return to_swap(orb_ref.at[y_peer(d)], ring.at[seat, stop, y], piece_ss, piece_rs, d)

    def idx_copy(d):
        return to_swap(idx_send, idx_all.at[y], idx_ss, idx_rs, d)

    @pl.when(moved)
    def _():
        piece_copy(0).start()

    for d in range(1, ny):
        piece_copy(d).start()

    lane = lax.broadcasted_iota(jnp.int32, idx_send.shape, 1)
    table = jnp.zeros(idx_send.shape, jnp.int32)
    for j in range(wanted):
        table = jnp.where(lane == j, pair_ref[0, j // slots, j % slots], table)
    idx_send[...] = table

    @pl.when(same)
    def _():
        idx_all[y] = table
        ring[seat, stop, y] = orb_ref[y]

    @pl.when(moved)
    def _():
        idx_copy(0).start()

    for d in range(1, ny):
        idx_copy(d).start()

    @pl.when(moved)
    def _():
        piece_copy(0).wait_recv()

    for d in range(1, ny):
        piece_copy(d).wait_recv()

    half = stops // 2
    width = ny // CHUNKS

    def block_at(way, step):
        return lax.rem(stop - step + stops, stops) if way == 0 else lax.rem(stop + step, stops)

    def z_copy(way, step, part):
        view = ring.at[kind, block_at(way, step), pl.ds(part * width, width)]
        return remote(
            view, view, z_ss.at[way, step, part], z_rs.at[way, step, part],
            y * nz + z_peer(1 if way == 0 else -1), row,
        )

    def sibling(d):
        return base + lax.rem(kind + d, group)

    def sib_copy(d, way, step, part):
        view = ring.at[kind, block_at(way, step + 1), pl.ds(part * width, width)]
        return remote(
            view, view, sib_ss.at[d - 1, way, step, part], sib_rs.at[d - 1, way, step, part],
            pb, sibling(d),
        )

    def own_copy(d):
        view = ring.at[kind, stop]
        return remote(view, view, own_ss.at[d - 1], own_rs.at[d - 1], pb, sibling(d))

    others = range(1, group)

    def last(way, part):
        return (part < CHUNKS // 2) == (way == 0)

    pairs = [(way, part) for part in range(CHUNKS) for way in range(2)]
    for way, part in pairs:
        if half > 1 or last(way, part):
            z_copy(way, 0, part).start()
    for d in others:
        own_copy(d).start()

    span, local = w_ref.shape[2] // rows, w_ref.shape[1]
    folds = LANES // (span - LANES)
    fold = local // folds
    for p in range(rows):
        split = p * span + LANES
        wsend[p, :, :local] = w_ref[:, :, p * span : split]
        rest = w_ref[:, :, split : (p + 1) * span].astype(jnp.float32)
        wsend[p, :, local:] = jnp.concatenate(
            [rest[:, f * fold : (f + 1) * fold] for f in range(folds)], axis=2
        ).astype(jnp.bfloat16)

    def w_copy(d):
        to = row_peer(d)
        return remote(wsend.at[to], wcol_ref.at[row], w_ss.at[d - 1], w_rs.at[d - 1], pb, to)

    for d in range(1, rows):
        w_copy(d).start()
    own_columns = pltpu.make_async_copy(wsend.at[row], wcol_ref.at[row], local_sem.at[0])
    own_columns.start()

    def z_step(step, carry):
        for way, part in pairs:
            z_copy(way, step - 1, part).wait_recv()
            z_copy(way, step, part).start()
            for d in others:
                sib_copy(d, way, step - 1, part).start()
        return carry

    if half > 1:
        lax.fori_loop(1, half - 1, z_step, 0)
        for way, part in pairs:
            z_copy(way, half - 2, part).wait_recv()
            if last(way, part):
                z_copy(way, half - 1, part).start()
            for d in others:
                sib_copy(d, way, half - 2, part).start()

    @pl.when(moved)
    def _():
        idx_copy(0).wait_recv()

    for d in range(1, ny):
        idx_copy(d).wait_recv()
    to_smem = pltpu.make_async_copy(idx_all, idx_smem, local_sem.at[1])
    to_smem.start()
    to_smem.wait()

    for way, part in pairs:
        if last(way, part):
            z_copy(way, half - 1, part).wait_recv()
            for d in others:
                sib_copy(d, way, half - 1, part).start()

    def sib_wait(step, carry):
        for way, part in pairs:
            for d in others:
                sib_copy(d, way, step, part).wait_recv()
        return carry

    if group > 1:
        for d in others:
            own_copy(d).wait_recv()
        lax.fori_loop(0, half - 1, sib_wait, 0)
        for way, part in pairs:
            if last(way, part):
                for d in others:
                    sib_copy(d, way, half - 1, part).wait_recv()

    def y_copy(d, j):
        return remote(
            chosen.at[d, j], full_ref.at[j, t_row, y], y_ss.at[d, j], y_rs.at[d, j],
            y_peer(d) * nz + t_z, t_row,
        )

    def listed(at, j):
        k = idx_smem[at, 0, j]
        k_z = lax.rem(k, nz)
        return ring[lax.rem(k_z, group), lax.div(k_z, group), lax.div(k, nz)]

    for j in range(wanted):
        for d in range(ny):
            chosen[d, j] = listed(y_peer(d), j)
        for d in range(1, ny):
            y_copy(d, j).start()

        @pl.when(moved)
        def _(j=j):
            y_copy(0, j).start()

        @pl.when(same)
        def _(j=j):
            full_ref[j, row, y] = chosen[0, j]

    other = 1 - core

    def at_x(d):
        return lax.rem(x + d + nx, nx) * CORES + core

    def x_copy(way, j):
        view = full_ref.at[j, row]
        return remote(
            view, view, x_ss.at[way, j], x_rs.at[way, j], pb, at_x(1 if way == 0 else -1)
        )

    def hop_copy(j):
        ahead = 1 if j % 2 == 0 else -1
        view = full_ref.at[j, at_x(-ahead)]
        return remote(view, view, hop_ss.at[j], hop_rs.at[j], pb, at_x(ahead))

    def core_copy(d, j):
        view = full_ref.at[j, at_x(d)]
        return remote(
            view, view, core_ss.at[d, j], core_rs.at[d, j], pb, x * CORES + other
        )

    for j in range(wanted):
        for d in range(1, ny):
            y_copy(d, j).wait_recv()

        @pl.when(moved)
        def _(j=j):
            y_copy(0, j).wait_recv()

        if nx == 4:
            for way in range(2):
                x_copy(way, j).start()
        core_copy(0, j).start()
    if nx == 4:
        for j in range(wanted):
            for way in (0, 1) if j % 2 == 0 else (1, 0):
                x_copy(way, j).wait_recv()
                if way == j % 2:
                    hop_copy(j).start()
                core_copy(3 if way == 0 else 1, j).start()
        for j in range(wanted):
            hop_copy(j).wait_recv()
            core_copy(2, j).start()
    for j in range(wanted):
        for d in range(nx):
            core_copy(d, j).wait_recv()

    own_columns.wait()
    for d in range(1, rows):
        w_copy(d).wait()
    @pl.when(moved)
    def _():
        piece_copy(0).wait_send()
        idx_copy(0).wait_send()
        for j in range(wanted):
            y_copy(0, j).wait_send()

    for d in others:
        own_copy(d).wait_send()
    for d in range(1, ny):
        piece_copy(d).wait_send()
        idx_copy(d).wait_send()
        for j in range(wanted):
            y_copy(d, j).wait_send()

    def z_drain(step, carry):
        for way, part in pairs:
            z_copy(way, step, part).wait_send()
            for d in others:
                sib_copy(d, way, step, part).wait_send()
        return carry

    lax.fori_loop(0, half - 1, z_drain, 0)
    for way, part in pairs:
        if last(way, part):
            z_copy(way, half - 1, part).wait_send()
            for d in others:
                sib_copy(d, way, half - 1, part).wait_send()
    for j in range(wanted):
        if nx == 4:
            for way in range(2):
                x_copy(way, j).wait_send()
            hop_copy(j).wait_send()
        for d in range(nx):
            core_copy(d, j).wait_send()


def gather(ny, pb_total, rows, pair_list, orbitals, w):
    nz, nx = pb_total // ny, rows // CORES
    slots = pair_list.shape[2]
    stops = nz // GROUP
    siblings = max(GROUP - 1, 1)
    piece, width = orbitals.shape[1:]
    span = w.shape[2] // rows
    packed = w.shape[1] * span // LANES
    dma = pltpu.SemaphoreType.DMA
    half = stops // 2
    vmem = pl.BlockSpec(memory_space=pltpu.VMEM)
    return pl.pallas_call(
        functools.partial(gather_kernel, ny, nz, nx, GROUP),
        out_shape=(
            jax.ShapeDtypeStruct((2 * slots, rows, ny, piece, width), jnp.bfloat16),
            jax.ShapeDtypeStruct((rows, 2, packed, LANES), jnp.bfloat16),
        ),
        in_specs=[pl.BlockSpec(memory_space=pltpu.SMEM), vmem, vmem],
        out_specs=(vmem, vmem),
        scratch_shapes=[
            pltpu.VMEM((GROUP, stops, ny, piece, width), jnp.bfloat16),
            pltpu.VMEM((ny, 2 * slots, piece, width), jnp.bfloat16),
            pltpu.VMEM((rows, 2, packed, LANES), jnp.bfloat16),
            pltpu.VMEM((8, 128), jnp.int32),
            pltpu.VMEM((ny, 8, 128), jnp.int32),
            pltpu.SMEM((ny, 8, 128), jnp.int32),
            dma((ny,)), dma((ny,)),
            dma((ny,)), dma((ny,)),
            dma((2, half, CHUNKS)), dma((2, half, CHUNKS)),
            dma((siblings, 2, half, CHUNKS)), dma((siblings, 2, half, CHUNKS)),
            dma((siblings,)), dma((siblings,)),
            dma((ny, 2 * slots)), dma((ny, 2 * slots)),
            dma((2, 2 * slots)), dma((2, 2 * slots)),
            dma((2 * slots,)), dma((2 * slots,)),
            dma((nx, 2 * slots)), dma((nx, 2 * slots)),
            dma((rows - 1,)), dma((rows - 1,)),
            dma((2,)),
        ],
        compiler_params=pltpu.CompilerParams(collective_id=0, has_side_effects=True, vmem_limit_bytes=16 << 20),
        name="gather_orbitals",
    )(pair_list, orbitals, w)


def dot_t(a, b):
    return lax.dot_general(a, b, (((1,), (1,)), ((), ())), preferred_element_type=jnp.float32)


def rotate(block):
    half = block.shape[1] // 2
    return jnp.concatenate([block[:, half:], -block[:, :half]], axis=1)


def columns_of(wcol_ref, p, part, local):
    first = wcol_ref[p, part, :local].astype(jnp.float32)
    rest = wcol_ref[p, part, local:].astype(jnp.float32)
    wide = local - LANES
    rest = jnp.concatenate(
        [rest[:, f * wide : (f + 1) * wide] for f in range(LANES // wide)], axis=0
    )
    return jnp.concatenate([first, rest], axis=1)


def exchange_kernel(flag_ref, count_ref, place_ref, full_ref, w_ref, wcol_ref, out_ref):
    slots, local, width = out_ref.shape
    rows = full_ref.shape[1]
    half = width // 2
    total = w_ref.shape[2]
    tile = 256
    me = place_ref[0]

    for s in range(slots):
        live = s < count_ref[0]
        adjoint = flag_ref[0, s] == 1

        @pl.when(jnp.logical_and(live, jnp.logical_not(adjoint)))
        def _(s=s):
            mine = full_ref[slots + s, pl.ds(pl.multiple_of(me * local, local), local), :]
            turned = rotate(mine)
            prod_re = jnp.zeros((local, width), jnp.float32)
            prod_im = jnp.zeros((local, width), jnp.float32)
            for c in range(total // tile):
                cols = pl.ds(c * tile, tile)
                source = full_ref[slots + s, cols, :]
                target = full_ref[s, cols, :]
                d_re = dot_t(mine, source)
                d_im = dot_t(turned, source)
                w_re = w_ref[0, :, cols].astype(jnp.float32)
                w_im = w_ref[1, :, cols].astype(jnp.float32)
                k_re = (w_re * d_re - w_im * d_im).astype(jnp.bfloat16)
                k_im = (w_re * d_im + w_im * d_re).astype(jnp.bfloat16)
                prod_re += jnp.dot(k_re, target, preferred_element_type=jnp.float32)
                prod_im += jnp.dot(k_im, target, preferred_element_type=jnp.float32)
            out_ref[s, :, :half] = prod_re[:, :half] - prod_im[:, half:]
            out_ref[s, :, half:] = prod_re[:, half:] + prod_im[:, :half]

        @pl.when(jnp.logical_and(live, adjoint))
        def _(s=s):
            mine = full_ref[slots + s, pl.ds(pl.multiple_of(me * local, local), local), :]
            prod_re = jnp.zeros((width, local), jnp.float32)
            prod_im = jnp.zeros((width, local), jnp.float32)
            for p in range(wcol_ref.shape[0]):
                cols = pl.ds(p * local, local)
                source = full_ref[slots + s, cols, :]
                target = full_ref[s, cols, :]
                d_re = dot_t(source, mine)
                d_im = dot_t(rotate(source), mine)
                w_re = columns_of(wcol_ref, p, 0, local)
                w_im = columns_of(wcol_ref, p, 1, local)
                k_re = (w_re * d_re - w_im * d_im).astype(jnp.bfloat16)
                k_im = (w_re * d_im + w_im * d_re).astype(jnp.bfloat16)
                flip = target.T
                prod_re += jnp.dot(flip, k_re, preferred_element_type=jnp.float32)
                prod_im += jnp.dot(flip, k_im, preferred_element_type=jnp.float32)
            top = prod_re[:half] + prod_im[half:]
            bottom = prod_re[half:] - prod_im[:half]
            out_ref[s] = jnp.concatenate([top, bottom], axis=0).T

        @pl.when(jnp.logical_not(live))
        def _(s=s):
            out_ref[s] = jnp.zeros((local, width), jnp.float32)


def exchange(flag_list, pair_counts, place, full, w, wcol):
    slots = full.shape[0] // 2
    local, width = w.shape[1], full.shape[2]
    smem = pl.BlockSpec(memory_space=pltpu.SMEM)
    vmem = pl.BlockSpec(memory_space=pltpu.VMEM)
    return pl.pallas_call(
        exchange_kernel,
        out_shape=jax.ShapeDtypeStruct((slots, local, width), jnp.float32),
        in_specs=[smem, smem, smem, vmem, vmem, vmem],
        out_specs=vmem,
        compiler_params=pltpu.CompilerParams(vmem_limit_bytes=16 << 20),
        name="exchange_terms",
    )(flag_list, pair_counts, place, full, w, wcol)


def shards(ny, pb_total, rows, orbitals, interaction, pair_list, flag_list, pair_counts):
    local, width = orbitals.shape[1:]
    w = interaction[:, 0]
    pieces = orbitals.reshape(ny, local // ny, width)
    pairs = jnp.transpose(pair_list, (0, 2, 1))
    full, wcol = gather(ny, pb_total, rows, pairs, pieces, w)
    full = full.reshape(full.shape[0], rows * local, width)
    place = lax.axis_index("row").astype(jnp.int32).reshape(1)
    return exchange(flag_list, pair_counts, place, full, w, wcol)[None]


def solution(mesh, ny=NY):
    return jax.shard_map(
        functools.partial(shards, ny, mesh.shape["pb"], mesh.shape["row"]),
        mesh=mesh,
        in_specs=(
            P("pb", "row", None),
            P(None, "pb", "row", None),
            P("pb", None, None),
            P("pb", None),
            P("pb"),
        ),
        out_specs=P("pb", None, "row", None),
        check_vma=False,
    )
```

time: 103 us -> 84.9 us (0.82)
  Pallas kernels: 101 us -> 79.6 us
  local copies, waits for them, and re-layouts: 1.34 us -> 4.39 us
    pallas_call x1, Pallas kernels: 94.3 us -> 74.9 us  [gather(): pl.pallas_call(functools.partial(gather_kernel, ny, nz, nx, GROUP), out_s...]
    unnamed x1 -> x10, local copies, waits for them, and re-layouts: 1.34 us -> 4.39 us
    pallas_call x1, Pallas kernels: 6.26 us -> 4.65 us  [exchange(): pl.pallas_call(exchange_kernel, out_shape=jax.ShapeDtypeStruct((slots, lo...]
where the time goes in v2:
time: 84.9 us; the launch traced here: 84.6 us
  Pallas kernels  79.6 us (94%)
  local copies, waits for them, and re-layouts  4.39 us (5%)
    pallas_call x1, Pallas kernels, gather(): pl.pallas_call(functools.partial(gather_kernel, ny, nz, nx, GROUP), out_s...  74.9 us
    pallas_call x1, Pallas kernels, exchange(): pl.pallas_call(exchange_kernel, out_shape=jax.ShapeDtypeStruct((slots, lo...  4.65 us
    unnamed x10, local copies, waits for them, and re-layouts  4.39 us

profile of v2, /device:TPU:1, one launch (start us, length us, event | category | flops | bytes accessed | tf_op | source)
XLA Modules:
  0.0 84.6 jit_solution(8537049811483992681)
XLA Ops:
  0.7 0.0 copy-start
  0.7 1.1 %copy-done = bf16[2,1,160,1280]{3,2,1,0:T(8,128)(2,1)S(1)} copy-done((bf16[2,1,160,1280]{3,2,1,0:T(8,128)(2,1)S(1)}, bf16[2,1,160,1280]{3,2,1,0:T(8,128)(2,1)}, u32[]{:S(2)}) %copy-start) | copy-done | bytes 819224
  1.8 0.0 copy-start.2
  1.8 0.8 copy-done.2
  2.6 0.0 copy-start.3
  2.6 0.7 copy-done.3
  3.3 74.9 %gather_orbitals.1 = (bf16[6,8,4,40,128]{4,3,2,1,0:T(8,128)(2,1)S(1)}, bf16[8,2,200,128]{3,2,1,0:T(8,128)(2,1)S(1)}) custom-call(s32[1,2,3]{2,1,0:T(2,128)S(1)} %bitcast.10, bf16[4,40,128]{2,1,0:T(8,128)(2,1)S(1)} %bitcast.9, bf16[2,160,1280]{2,1,0:T(8,128)(2,1)S(1)} %bitcast.6), custom_call_target="tpu_custom_call" | custom-call | tf_op jit(solution)/shard_map/gather_orbitals/pallas_call | solution.py:347
  78.2 0.0 copy-start.1
  78.2 1.1 %copy-done.1 = bf16[2,1,160,1280]{3,2,1,0:T(8,128)(2,1)S(1)} copy-done((bf16[2,1,160,1280]{3,2,1,0:T(8,128)(2,1)S(1)}, bf16[2,1,160,1280]{3,2,1,0:T(8,128)(2,1)}, u32[]{:S(2)}) %copy-start.1) | copy-done | bytes 819224
  79.3 0.0 copy-start.4
  79.3 0.7 copy-done.4
  80.0 4.7 %exchange_terms.1 = f32[3,160,128]{2,1,0:T(8,128)} custom-call(s32[1,3]{1,0:T(1,128)S(1)} %copy-done.4, s32[1]{0:T(128)S(6)} %copy.6.count_ref, s32[1]{0:T(128)} %bitcast.place_ref, bf16[6,1280,128]{2,1,0:T(8,128)(2,1)S(1)} %bitcast.8, bf16[2,160,1280]{2,1,0:T(8,128)(2,1)S(1)} %bitcast.7, bf16[8,2,200,128]{3,2,1,0:T(8,128)(2,1)S(1)} %get-tuple-element.8.wcol_ref), custom_call_target="tpu_custom_call" | custom-call | tf_op jit(solution)/shard_map/exchange_terms/pallas_call | solution.py:463
Async XLA Ops:
  0.7 1.1 %copy-start = (bf16[2,1,160,1280]{3,2,1,0:T(8,128)(2,1)S(1)}, bf16[2,1,160,1280]{3,2,1,0:T(8,128)(2,1)}, u32[]{:S(2)}) copy-start(bf16[2,1,160,1280]{3,2,1,0:T(8,128)(2,1)} %param.6) | copy-start | bytes 2457604
  1.8 0.8 copy-start.2
  2.6 0.7 copy-start.3
  78.2 1.1 %copy-start.1 = (bf16[2,1,160,1280]{3,2,1,0:T(8,128)(2,1)S(1)}, bf16[2,1,160,1280]{3,2,1,0:T(8,128)(2,1)}, u32[]{:S(2)}) copy-start(bf16[2,1,160,1280]{3,2,1,0:T(8,128)(2,1)} %param.6) | copy-start | bytes 2457604
  79.3 0.7 copy-start.4

commit v3 on v2

--- a/solution.py
+++ b/solution.py
@@ -17,9 +17,9 @@
 
 def gather_kernel(
     ny, nz, nx, group,
-    pair_ref, orb_ref, w_ref,
-    full_ref, wcol_ref,
-    ring, chosen, wsend, idx_send, idx_all, idx_smem,
+    pair_hbm, orb_ref, w_hbm,
+    full_ref, wcol_ref, w_ref,
+    ring, chosen, wsend, idx_send, idx_all, idx_smem, pair_ref,
     idx_ss, idx_rs, piece_ss, piece_rs, z_ss, z_rs, sib_ss, sib_rs, own_ss, own_rs, y_ss, y_rs,
     x_ss, x_rs, hop_ss, hop_rs, core_ss, core_rs, w_ss, w_rs, local_sem,
 ):
@@ -53,9 +53,14 @@
             device_id=(to_pb, to_row), device_id_type=MESH,
         )
 
+    pair_load = pltpu.make_async_copy(pair_hbm, pair_ref, local_sem.at[2])
+    pair_load.start()
+    w_load = pltpu.make_async_copy(w_hbm, w_ref, local_sem.at[3])
+    own_piece = pltpu.make_async_copy(orb_ref.at[y], ring.at[seat, stop, y], local_sem.at[4])
+
     barrier = pltpu.get_barrier_semaphore()
     partners = [(y_peer(d) * nz + t_z, t_row) for d in range(1, ny)]
-    ways = (1, -1) if stops > 2 else (1,)
+    ways = (1, -1, 2, -2)
     partners += [(y * nz + z_peer(d), row) for d in ways]
     partners += [(pb, row_peer(d)) for d in range(1, rows)]
     for partner in partners:
@@ -88,6 +93,12 @@
     for d in range(1, ny):
         piece_copy(d).start()
 
+    @pl.when(same)
+    def _():
+        own_piece.start()
+
+    w_load.start()
+    pair_load.wait()
     lane = lax.broadcasted_iota(jnp.int32, idx_send.shape, 1)
     table = jnp.zeros(idx_send.shape, jnp.int32)
     for j in range(wanted):
@@ -97,7 +108,6 @@
     @pl.when(same)
     def _():
         idx_all[y] = table
-        ring[seat, stop, y] = orb_ref[y]
 
     @pl.when(moved)
     def _():
@@ -106,6 +116,10 @@
     for d in range(1, ny):
         idx_copy(d).start()
 
+    @pl.when(same)
+    def _():
+        own_piece.wait()
+
     @pl.when(moved)
     def _():
         piece_copy(0).wait_recv()
@@ -119,20 +133,21 @@
     def block_at(way, step):
         return lax.rem(stop - step + stops, stops) if way == 0 else lax.rem(stop + step, stops)
 
-    def z_copy(way, step, part):
+    def z_copy(way, gone, part):
+        hop = 2 - lax.rem(gone, 2)
+        view = ring.at[kind, block_at(way, gone - hop), pl.ds(part * width, width)]
+        return remote(
+            view, view, z_ss.at[way, gone - 1, part], z_rs.at[way, gone - 1, part],
+            y * nz + z_peer(hop if way == 0 else -hop), row,
+        )
+
+    def sibling(d):
+        return base + lax.rem(kind + d, group)
+
+    def sib_copy(d, way, step, part):
         view = ring.at[kind, block_at(way, step), pl.ds(part * width, width)]
         return remote(
-            view, view, z_ss.at[way, step, part], z_rs.at[way, step, part],
-            y * nz + z_peer(1 if way == 0 else -1), row,
-        )
-
-    def sibling(d):
-        return base + lax.rem(kind + d, group)
-
-    def sib_copy(d, way, step, part):
-        view = ring.at[kind, block_at(way, step + 1), pl.ds(part * width, width)]
-        return remote(
-            view, view, sib_ss.at[d - 1, way, step, part], sib_rs.at[d - 1, way, step, part],
+            view, view, sib_ss.at[d - 1, way, step - 1, part], sib_rs.at[d - 1, way, step - 1, part],
             pb, sibling(d),
         )
 
@@ -146,15 +161,16 @@
         return (part < CHUNKS // 2) == (way == 0)
 
     pairs = [(way, part) for part in range(CHUNKS) for way in range(2)]
-    for way, part in pairs:
-        if half > 1 or last(way, part):
-            z_copy(way, 0, part).start()
+    for hop in (1, 2):
+        for way, part in pairs:
+            z_copy(way, hop, part).start()
     for d in others:
         own_copy(d).start()
 
     span, local = w_ref.shape[2] // rows, w_ref.shape[1]
     folds = LANES // (span - LANES)
     fold = local // folds
+    w_load.wait()
     for p in range(rows):
         split = p * span + LANES
         wsend[p, :, :local] = w_ref[:, :, p * span : split]
@@ -172,22 +188,33 @@
     own_columns = pltpu.make_async_copy(wsend.at[row], wcol_ref.at[row], local_sem.at[0])
     own_columns.start()
 
+    def to_siblings(way, gone, part):
+        for d in others:
+            sib_copy(d, way, gone, part).start()
+
     def z_step(step, carry):
-        for way, part in pairs:
-            z_copy(way, step - 1, part).wait_recv()
-            z_copy(way, step, part).start()
-            for d in others:
-                sib_copy(d, way, step - 1, part).start()
+        gone = 2 * step
+        for way, part in pairs:
+            z_copy(way, gone, part).wait_recv()
+            z_copy(way, gone + 2, part).start()
+            z_copy(way, gone + 1, part).start()
+            to_siblings(way, gone, part)
+        for way, part in pairs:
+            z_copy(way, gone - 1, part).wait_recv()
+            to_siblings(way, gone - 1, part)
         return carry
 
-    if half > 1:
-        lax.fori_loop(1, half - 1, z_step, 0)
-        for way, part in pairs:
-            z_copy(way, half - 2, part).wait_recv()
-            if last(way, part):
-                z_copy(way, half - 1, part).start()
-            for d in others:
-                sib_copy(d, way, half - 2, part).start()
+    lax.fori_loop(1, half // 2 - 1, z_step, 0)
+    for way, part in pairs:
+        z_copy(way, half - 2, part).wait_recv()
+        if last(way, part):
+            z_copy(way, half, part).start()
+        z_copy(way, half - 1, part).start()
+        to_siblings(way, half - 2, part)
+    for gone in (half - 3, half - 1):
+        for way, part in pairs:
+            z_copy(way, gone, part).wait_recv()
+            to_siblings(way, gone, part)
 
     @pl.when(moved)
     def _():
@@ -201,9 +228,8 @@
 
     for way, part in pairs:
         if last(way, part):
-            z_copy(way, half - 1, part).wait_recv()
-            for d in others:
-                sib_copy(d, way, half - 1, part).start()
+            z_copy(way, half, part).wait_recv()
+            to_siblings(way, half, part)
 
     def sib_wait(step, carry):
         for way, part in pairs:
@@ -214,11 +240,11 @@
     if group > 1:
         for d in others:
             own_copy(d).wait_recv()
-        lax.fori_loop(0, half - 1, sib_wait, 0)
+        lax.fori_loop(1, half, sib_wait, 0)
         for way, part in pairs:
             if last(way, part):
                 for d in others:
-                    sib_copy(d, way, half - 1, part).wait_recv()
+                    sib_copy(d, way, half, part).wait_recv()
 
     def y_copy(d, j):
         return remote(
@@ -318,12 +344,12 @@
                 sib_copy(d, way, step, part).wait_send()
         return carry
 
-    lax.fori_loop(0, half - 1, z_drain, 0)
+    lax.fori_loop(1, half, z_drain, 0)
     for way, part in pairs:
         if last(way, part):
-            z_copy(way, half - 1, part).wait_send()
+            z_copy(way, half, part).wait_send()
             for d in others:
-                sib_copy(d, way, half - 1, part).wait_send()
+                sib_copy(d, way, half, part).wait_send()
     for j in range(wanted):
         if nx == 4:
             for way in range(2):
@@ -349,9 +375,10 @@
         out_shape=(
             jax.ShapeDtypeStruct((2 * slots, rows, ny, piece, width), jnp.bfloat16),
             jax.ShapeDtypeStruct((rows, 2, packed, LANES), jnp.bfloat16),
+            jax.ShapeDtypeStruct(w.shape, w.dtype),
         ),
-        in_specs=[pl.BlockSpec(memory_space=pltpu.SMEM), vmem, vmem],
-        out_specs=(vmem, vmem),
+        in_specs=[pl.BlockSpec(memory_space=pltpu.HBM)] * 3,
+        out_specs=(vmem, vmem, vmem),
         scratch_shapes=[
             pltpu.VMEM((GROUP, stops, ny, piece, width), jnp.bfloat16),
             pltpu.VMEM((ny, 2 * slots, piece, width), jnp.bfloat16),
@@ -359,6 +386,7 @@
             pltpu.VMEM((8, 128), jnp.int32),
             pltpu.VMEM((ny, 8, 128), jnp.int32),
             pltpu.SMEM((ny, 8, 128), jnp.int32),
+            pltpu.SMEM(pair_list.shape, jnp.int32),
             dma((ny,)), dma((ny,)),
             dma((ny,)), dma((ny,)),
             dma((2, half, CHUNKS)), dma((2, half, CHUNKS)),
@@ -369,11 +397,11 @@
             dma((2 * slots,)), dma((2 * slots,)),
             dma((nx, 2 * slots)), dma((nx, 2 * slots)),
             dma((rows - 1,)), dma((rows - 1,)),
-            dma((2,)),
+            dma((5,)),
         ],
         compiler_params=pltpu.CompilerParams(collective_id=0, has_side_effects=True, vmem_limit_bytes=16 << 20),
         name="gather_orbitals",
-    )(pair_list, orbitals, w)
+    )(*(pltpu.with_memory_space_constraint(a, pltpu.HBM) for a in (pair_list, orbitals, w)))
 
 
 def dot_t(a, b):
@@ -475,7 +503,7 @@
     w = interaction[:, 0]
     pieces = orbitals.reshape(ny, local // ny, width)
     pairs = jnp.transpose(pair_list, (0, 2, 1))
-    full, wcol = gather(ny, pb_total, rows, pairs, pieces, w)
+    full, wcol, w = gather(ny, pb_total, rows, pairs, pieces, w)
     full = full.reshape(full.shape[0], rows * local, width)
     place = lax.axis_index("row").astype(jnp.int32).reshape(1)
     return exchange(flag_list, pair_counts, place, full, w, wcol)[None]

time: 84.9 us -> 77.8 us (0.916)
  local copies, waits for them, and re-layouts: 4.39 us -> 0.65 us
  Pallas kernels: 79.6 us -> 76.3 us
    unnamed x10 -> x2, local copies, waits for them, and re-layouts: 4.39 us -> 0.65 us
    pallas_call x1, Pallas kernels: 74.9 us -> 71.8 us  [gather(): pl.pallas_call(functools.partial(gather_kernel, ny, nz, nx, GROUP), out_s...]
where the time goes in v3:
time: 77.8 us; the launch traced here: 77.6 us
  Pallas kernels  76.3 us (98%)
    pallas_call x1, Pallas kernels, gather(): pl.pallas_call(functools.partial(gather_kernel, ny, nz, nx, GROUP), out_s...  71.8 us
    pallas_call x1, Pallas kernels, exchange(): pl.pallas_call(exchange_kernel, out_shape=jax.ShapeDtypeStruct((slots, lo...  4.56 us

profile of v3, /device:TPU:1, one launch (start us, length us, event | category | flops | bytes accessed | tf_op | source)
XLA Modules:
  0.0 77.6 jit_solution(3553551795834623477)
XLA Ops:
  0.7 71.8 %gather_orbitals.1 = (bf16[6,8,4,40,128]{4,3,2,1,0:T(8,128)(2,1)S(1)}, bf16[8,2,200,128]{3,2,1,0:T(8,128)(2,1)S(1)}, bf16[2,160,1280]{2,1,0:T(8,128)(2,1)S(1)}) custom-call(s32[1,2,3]{2,1,0:T(2,128)} %bitcast.9, bf16[4,40,128]{2,1,0:T(8,128)(2,1)} %bitcast.8, bf16[2,160,1280]{2,1,0:T(8,128)(2,1)} %bitcast.7), custom_call_target="tpu_custom_call" | custom-call | tf_op jit(solution)/shard_map/gather_orbitals/pallas_call | solution.py:373
  72.4 0.0 copy-start
  72.4 0.6 copy-done
  73.1 4.6 %exchange_terms.1 = f32[3,160,128]{2,1,0:T(8,128)} custom-call(s32[1,3]{1,0:T(1,128)S(1)} %copy-done, s32[1]{0:T(128)S(6)} %copy.6.count_ref, s32[1]{0:T(128)} %bitcast.place_ref, bf16[6,1280,128]{2,1,0:T(8,128)(2,1)S(1)} %bitcast.6, bf16[2,160,1280]{2,1,0:T(8,128)(2,1)S(1)} %get-tuple-element.9.w_ref, bf16[8,2,200,128]{3,2,1,0:T(8,128)(2,1)S(1)} %get-tuple-element.10.wcol_ref), custom_call_target="tpu_custom_call" | custom-call | tf_op jit(solution)/shard_map/exchange_terms/pallas_call | solution.py:491
Async XLA Ops:
  72.4 0.7 copy-start

commit v4 on v3

--- a/solution.py
+++ b/solution.py
@@ -161,7 +161,7 @@
         return (part < CHUNKS // 2) == (way == 0)
 
     pairs = [(way, part) for part in range(CHUNKS) for way in range(2)]
-    for hop in (1, 2):
+    for hop in (2, 1):
         for way, part in pairs:
             z_copy(way, hop, part).start()
     for d in others:
@@ -197,6 +197,7 @@
         for way, part in pairs:
             z_copy(way, gone, part).wait_recv()
             z_copy(way, gone + 2, part).start()
+        for way, part in pairs:
             z_copy(way, gone + 1, part).start()
             to_siblings(way, gone, part)
         for way, part in pairs:
@@ -260,7 +261,7 @@
     for j in range(wanted):
         for d in range(ny):
             chosen[d, j] = listed(y_peer(d), j)
-        for d in range(1, ny):
+        for d in sorted(range(1, ny), key=lambda d: -min(d, ny - d)):
             y_copy(d, j).start()
 
         @pl.when(moved)
@@ -438,21 +439,21 @@
         @pl.when(jnp.logical_and(live, jnp.logical_not(adjoint)))
         def _(s=s):
             mine = full_ref[slots + s, pl.ds(pl.multiple_of(me * local, local), local), :]
-            turned = rotate(mine)
-            prod_re = jnp.zeros((local, width), jnp.float32)
-            prod_im = jnp.zeros((local, width), jnp.float32)
+            both = jnp.concatenate([mine, rotate(mine)], axis=0)
+            prod = jnp.zeros((2 * local, width), jnp.float32)
             for c in range(total // tile):
                 cols = pl.ds(c * tile, tile)
                 source = full_ref[slots + s, cols, :]
                 target = full_ref[s, cols, :]
-                d_re = dot_t(mine, source)
-                d_im = dot_t(turned, source)
+                dens = dot_t(both, source)
+                d_re, d_im = dens[:local], dens[local:]
                 w_re = w_ref[0, :, cols].astype(jnp.float32)
                 w_im = w_ref[1, :, cols].astype(jnp.float32)
                 k_re = (w_re * d_re - w_im * d_im).astype(jnp.bfloat16)
                 k_im = (w_re * d_im + w_im * d_re).astype(jnp.bfloat16)
-                prod_re += jnp.dot(k_re, target, preferred_element_type=jnp.float32)
-                prod_im += jnp.dot(k_im, target, preferred_element_type=jnp.float32)
+                kern = jnp.concatenate([k_re, k_im], axis=0)
+                prod += jnp.dot(kern, target, preferred_element_type=jnp.float32)
+            prod_re, prod_im = prod[:local], prod[local:]
             out_ref[s, :, :half] = prod_re[:, :half] - prod_im[:, half:]
             out_ref[s, :, half:] = prod_re[:, half:] + prod_im[:, :half]
 
@@ -495,7 +496,10 @@
         out_specs=vmem,
         compiler_params=pltpu.CompilerParams(vmem_limit_bytes=16 << 20),
         name="exchange_terms",
-    )(flag_list, pair_counts, place, full, w, wcol)
+    )(
+        pltpu.with_memory_space_constraint(flag_list, pltpu.HBM),
+        pair_counts, place, full, w, wcol,
+    )
 
 
 def shards(ny, pb_total, rows, orbitals, interaction, pair_list, flag_list, pair_counts):

time: 77.8 us -> 75.8 us (0.974)
  Pallas kernels: 76.3 us -> 75.2 us
    pallas_call x1, Pallas kernels: 71.8 us -> 70.4 us  [gather(): pl.pallas_call(functools.partial(gather_kernel, ny, nz, nx, GROUP), out_s...]
where the time goes in v4:
time: 75.8 us; the launch traced here: 75.9 us
  Pallas kernels  75.2 us (99%)
    pallas_call x1, Pallas kernels, gather(): pl.pallas_call(functools.partial(gather_kernel, ny, nz, nx, GROUP), out_s...  70.4 us
    pallas_call x1, Pallas kernels, exchange(): pl.pallas_call(exchange_kernel, out_shape=jax.ShapeDtypeStruct((slots, lo...  4.81 us

profile of v4, /device:TPU:1, one launch (start us, length us, event | category | flops | bytes accessed | tf_op | source)
XLA Modules:
  0.0 75.9 jit_solution(14021665173597169072)
XLA Ops:
  0.7 70.4 %gather_orbitals.1 = (bf16[6,8,4,40,128]{4,3,2,1,0:T(8,128)(2,1)S(1)}, bf16[8,2,200,128]{3,2,1,0:T(8,128)(2,1)S(1)}, bf16[2,160,1280]{2,1,0:T(8,128)(2,1)S(1)}) custom-call(s32[1,2,3]{2,1,0:T(2,128)} %bitcast.9, bf16[4,40,128]{2,1,0:T(8,128)(2,1)} %bitcast.8, bf16[2,160,1280]{2,1,0:T(8,128)(2,1)} %bitcast.7), custom_call_target="tpu_custom_call" | custom-call | tf_op jit(solution)/shard_map/gather_orbitals/pallas_call | solution.py:374
  71.1 4.8 %exchange_terms.1 = f32[3,160,128]{2,1,0:T(8,128)} custom-call(s32[1,3]{1,0:T(1,128)} %flag_ref.1, s32[1]{0:T(128)S(6)} %copy.6.count_ref, s32[1]{0:T(128)} %bitcast.place_ref, bf16[6,1280,128]{2,1,0:T(8,128)(2,1)S(1)} %bitcast.6, bf16[2,160,1280]{2,1,0:T(8,128)(2,1)S(1)} %get-tuple-element.9.w_ref, bf16[8,2,200,128]{3,2,1,0:T(8,128)(2,1)S(1)} %get-tuple-element.10.wcol_ref), custom_call_target="tpu_custom_call" | custom-call | tf_op jit(solution)/shard_map/exchange_terms/pallas_call | solution.py:492

commit v5 on v4

--- a/solution.py
+++ b/solution.py
@@ -188,6 +188,15 @@
     own_columns = pltpu.make_async_copy(wsend.at[row], wcol_ref.at[row], local_sem.at[0])
     own_columns.start()
 
+    @pl.when(moved)
+    def _():
+        idx_copy(0).wait_recv()
+
+    for d in range(1, ny):
+        idx_copy(d).wait_recv()
+    to_smem = pltpu.make_async_copy(idx_all, idx_smem, local_sem.at[1])
+    to_smem.start()
+
     def to_siblings(way, gone, part):
         for d in others:
             sib_copy(d, way, gone, part).start()
@@ -217,14 +226,6 @@
             z_copy(way, gone, part).wait_recv()
             to_siblings(way, gone, part)
 
-    @pl.when(moved)
-    def _():
-        idx_copy(0).wait_recv()
-
-    for d in range(1, ny):
-        idx_copy(d).wait_recv()
-    to_smem = pltpu.make_async_copy(idx_all, idx_smem, local_sem.at[1])
-    to_smem.start()
     to_smem.wait()
 
     for way, part in pairs:
@@ -466,8 +467,9 @@
                 cols = pl.ds(p * local, local)
                 source = full_ref[slots + s, cols, :]
                 target = full_ref[s, cols, :]
-                d_re = dot_t(source, mine)
-                d_im = dot_t(rotate(source), mine)
+                both = jnp.concatenate([source, rotate(source)], axis=0)
+                dens = dot_t(both, mine)
+                d_re, d_im = dens[:local], dens[local:]
                 w_re = columns_of(wcol_ref, p, 0, local)
                 w_im = columns_of(wcol_ref, p, 1, local)
                 k_re = (w_re * d_re - w_im * d_im).astype(jnp.bfloat16)

time: 75.8 us -> 75.8 us (level)
  no operation moved by 1% of the time
where the time goes in v5:
time: 75.8 us; the launch traced here: 75.6 us
  Pallas kernels  75 us (99%)
    pallas_call x1, Pallas kernels, gather(): pl.pallas_call(functools.partial(gather_kernel, ny, nz, nx, GROUP), out_s...  70.4 us
    pallas_call x1, Pallas kernels, exchange(): pl.pallas_call(exchange_kernel, out_shape=jax.ShapeDtypeStruct((slots, lo...  4.6 us

profile of v5, /device:TPU:1, one launch (start us, length us, event | category | flops | bytes accessed | tf_op | source)
XLA Modules:
  0.0 75.6 jit_solution(3500174881268214645)
XLA Ops:
  0.7 70.4 %gather_orbitals.1 = (bf16[6,8,4,40,128]{4,3,2,1,0:T(8,128)(2,1)S(1)}, bf16[8,2,200,128]{3,2,1,0:T(8,128)(2,1)S(1)}, bf16[2,160,1280]{2,1,0:T(8,128)(2,1)S(1)}) custom-call(s32[1,2,3]{2,1,0:T(2,128)} %bitcast.9, bf16[4,40,128]{2,1,0:T(8,128)(2,1)} %bitcast.8, bf16[2,160,1280]{2,1,0:T(8,128)(2,1)} %bitcast.7), custom_call_target="tpu_custom_call" | custom-call | tf_op jit(solution)/shard_map/gather_orbitals/pallas_call | solution.py:375
  71.1 4.6 %exchange_terms.1 = f32[3,160,128]{2,1,0:T(8,128)} custom-call(s32[1,3]{1,0:T(1,128)} %flag_ref.1, s32[1]{0:T(128)S(6)} %copy.6.count_ref, s32[1]{0:T(128)} %bitcast.place_ref, bf16[6,1280,128]{2,1,0:T(8,128)(2,1)S(1)} %bitcast.6, bf16[2,160,1280]{2,1,0:T(8,128)(2,1)S(1)} %get-tuple-element.9.w_ref, bf16[8,2,200,128]{3,2,1,0:T(8,128)(2,1)S(1)} %get-tuple-element.10.wcol_ref), custom_call_target="tpu_custom_call" | custom-call | tf_op jit(solution)/shard_map/exchange_terms/pallas_call | solution.py:494
